TPU v7x, 256 devices: a whole 4x4x8 slice. The times are simulated.
256 devices in a mesh: gx: 4 (over y), gy: 8 (over x, core), gz: 8 (over z).
Axes of the slice: x: 4, y: 4, z: 8, core: 2. Of those that a mesh axis runs over, the one named last changes fastest.
Arguments:
- basis: bfloat16 [8, 3, 64, 1024, 128], P('gx', None, 'gy', 'gz'), may hold values from -4.8 to 4.8
- modal_now: bfloat16 [128, 8], replicated, may hold values from -0.5 to 0.5
- modal_prev: bfloat16 [128, 8], replicated, may hold values from -0.5 to 0.5
- material_ids: int32 [8, 64, 1024], P('gx', 'gy', 'gz'), may hold values from 0 to 3
- moduli: float32 [3, 4], replicated, may hold values from 0.4 to 1.6
- drive_mask: int32 [8, 8, 64, 1024], P(None, 'gx', 'gy', 'gz'), may hold values 0 or 1
- drive: float32 [3, 8], replicated, may hold values from -8 to 8
Outputs:
- displacement: float32 [3, 8, 8, 64, 1024], P(None, None, 'gx', 'gy', 'gz')
- modes: float32 [3, 8, 8, 64, 1024], P(None, None, 'gx', 'gy', 'gz')
- coefficients: float32 [4, 2, 128, 8], replicated
- rfactor: float32 [4, 8, 8], replicated
All inputs are finite; a program needn't handle non-finite values. No bound on the sum of `drive_mask` on one device may be relied on, other than what follows from the above.
Results may differ from a plain program's by a relative error of at most 0.0008.
The roundings to bfloat16 on the way count: a program that leaves them out, or rounds other values in their place, can miss the bound.
Values sent between devices are 32-bit elements; how exact they have to be, the bound alone decides.
No kernel may reach another device: no remote copies, remote signals or barrier semaphores. Data moves between devices by JAX's collectives and lax.ppermute only.
A program may use at most 128 MiB of HBM per device.

v0:
```python
import jax
import jax.numpy as jnp
from jax import lax
from jax.sharding import PartitionSpec as P

STEPS = 4
step_squared = 0.1
ramp_steps = 4.0


def padded_2(block, sides, width):
    for axis, dim in sides:
        count = lax.axis_size(axis)
        forward = [(i, i + 1) for i in range(count - 1)]
        backward = [(target, source) for source, target in forward]
        low = lax.ppermute(
            lax.slice_in_dim(block, block.shape[dim] - width, None, axis=dim), axis, forward
        )
        high = lax.ppermute(lax.slice_in_dim(block, 0, width, axis=dim), axis, backward)
        block = jnp.concatenate([low, block, high], axis=dim)
    return block


def interior(array, direction_axis, offset):
    base_axis = array.ndim - 3
    result = array
    for axis_index in range(3):
        extent = array.shape[base_axis + axis_index]
        begin = offset if axis_index == direction_axis else 1
        result = lax.slice_in_dim(result, begin, extent - 2 + begin, axis=base_axis + axis_index)
    return result


def stiffness(field, material_props):
    component_rows = []
    for component in range(3):
        center = interior(field[component], 0, 1)
        accumulated = jnp.zeros_like(center)
        for direction_axis in range(3):
            modulus = material_props[0] if component == direction_axis else material_props[1]
            center_modulus = interior(modulus, 0, 1)
            for offset in (0, 2):
                coupling = 0.5 * (center_modulus + interior(modulus, direction_axis, offset))
                accumulated = accumulated + coupling * (
                    center - interior(field[component], direction_axis, offset)
                )
        component_rows.append(accumulated)
    return jnp.stack(component_rows)


def lookup(material_ids, moduli):
    levels = jnp.arange(moduli.shape[1], dtype=jnp.int32)
    onehot = (material_ids[None] == levels[:, None, None, None]).astype(jnp.float32)
    return jnp.einsum("mxyz,pm->pxyz", onehot, moduli, precision=lax.Precision.HIGHEST)


def expand(basis, coefficient):
    return jnp.einsum("xcyzk,kj->cjxyz", basis, coefficient, preferred_element_type=jnp.float32)


def project(basis, field):
    return jnp.einsum("xcyzk,cjxyz->kj", basis, field, preferred_element_type=jnp.float32)


def apply_inverse(block, lower_factor):
    identity_block = jnp.eye(lower_factor.shape[0], dtype=jnp.float32)
    lower_inverse = jax.scipy.linalg.solve_triangular(lower_factor, identity_block, lower=True)
    return jnp.einsum("cixyz,ji->cjxyz", block, lower_inverse, precision=lax.Precision.HIGHEST)


def local_gram(block):
    return jnp.einsum("cixyz,cjxyz->ij", block, block, precision=lax.Precision.HIGHEST)


def orthonormalize(following, basis, dof_weight):
    highest = lax.Precision.HIGHEST
    snapshot = following.astype(jnp.bfloat16)
    partial_coef = project(basis, snapshot) * dof_weight
    first_coef = lax.psum(partial_coef, ("gx", "gy", "gz"))
    first_resid = snapshot.astype(jnp.float32) - expand(basis, first_coef.astype(jnp.bfloat16))
    first_gram = lax.psum(local_gram(first_resid) * dof_weight, ("gx", "gy", "gz"))
    first_lower = jnp.linalg.cholesky(first_gram)
    first_q = apply_inverse(first_resid, first_lower)
    second_coef = lax.psum(
        project(basis, first_q.astype(jnp.bfloat16)) * dof_weight, ("gx", "gy", "gz")
    )
    second_resid = first_q - expand(basis, second_coef.astype(jnp.bfloat16))
    second_gram = lax.psum(local_gram(second_resid) * dof_weight, ("gx", "gy", "gz"))
    second_lower = jnp.linalg.cholesky(second_gram)
    modes = apply_inverse(second_resid, second_lower)
    factor = jnp.dot(first_lower, second_lower, precision=highest).T
    return (jnp.stack([first_coef, second_coef]), factor, modes)


def shards(basis, modal_now, modal_prev, material_ids, moduli, drive_mask, drive):
    devices_total = lax.axis_size("gx") * lax.axis_size("gy") * lax.axis_size("gz")
    dof_weight = 1.0 / (3.0 * basis.shape[0] * basis.shape[2] * basis.shape[3] * devices_total)
    current = expand(basis, modal_now)
    earlier = expand(basis, modal_prev)
    material_props = lookup(material_ids, moduli)
    port_mask = drive_mask.astype(jnp.float32)
    static = jnp.concatenate([material_props, port_mask], axis=0)
    wide_static = padded_2(static, (("gx", 1), ("gy", 2), ("gz", 3)), 2)
    props_wide = wide_static[:3]
    props_near = props_wide[:, 1:-1, 1:-1, 1:-1]
    inverse_mass = material_props[2]
    drive_field = drive[:, :, None, None, None]
    coefficient_list = []
    factor_list = []
    modes = current
    for step in range(STEPS):
        padded = padded_2(current, (("gx", 2), ("gy", 3), ("gz", 4)), 1)
        ramp_level = min(1.0, (step + 1) / ramp_steps)
        load_field = drive_field * port_mask[None] * ramp_level
        following = (
            2.0 * current
            - earlier
            + step_squared * inverse_mass * (load_field - stiffness(padded, props_near))
        )
        earlier = current
        current = following
        coefs, factor, modes = orthonormalize(following, basis, dof_weight)
        coefficient_list.append(coefs)
        factor_list.append(factor)
    return (current, modes, jnp.stack(coefficient_list), jnp.stack(factor_list))


def solution(mesh):
    in_specs = (
        P("gx", None, "gy", "gz", None),
        P(),
        P(),
        P("gx", "gy", "gz"),
        P(),
        P(None, "gx", "gy", "gz"),
        P(),
    )
    out_specs = (P(None, None, "gx", "gy", "gz"), P(None, None, "gx", "gy", "gz"), P(), P())
    return jax.shard_map(shards, mesh=mesh, in_specs=in_specs, out_specs=out_specs, check_vma=False)
```

profile of v0, /device:TPU:1, one launch (start us, length us, event | category | flops | bytes accessed | tf_op | source)
XLA Modules:
  0.0 537.8 jit_solution(7000948003984317785)
XLA Ops:
  2.5 4.0 collective-permute-start
  9.1 4.0 collective-permute-start.6
  14.7 3.7 collective-permute-done.7
  18.5 5.7 %collective-permute-start.8 = (f32[3,8,4,1,128]{4,1,3,2,0:T(8,128)S(1)}, f32[3,8,4,1,128]{4,1,3,2,0:T(8,128)S(1)}, u32[]{:S(2)}, u32[]{:S(2)}) collective-permute-start(f32[3,8,4,1,128]{4,1,3,2,0:T(8,128)S(1)} %get-tuple-element.78), channel_id=1, source_target_pairs={{0,8},{8,16},{16,24},{24,32},{32,40},{40,48},{48,56},{1,9},{9,17},... | collective-permute-start | bytes 147464 | tf_op jit(solution)/shard_map/ppermute | solution.py:16
  30.7 3.6 collective-permute-start.10
  35.7 3.8 copy.222
  49.6 4.5 copy.221
  54.1 3.9 copy.223
  58.0 9.0 %pad_maximum_fusion = f32[11,6,12,128]{2,1,3,0:T(8,128)S(1)} fusion(f32[11,6,2,128]{2,1,3,0:T(8,128)} %copy.223, f32[11,6,8,128]{2,1,3,0:T(8,128)} %copy.222, f32[11,6,2,128]{2,1,3,0:T(8,128)} %copy.221), kind=kLoop, calls=%fused_computation | loop fusion | flops 202752 | bytes 811008 | tf_op jit(solution)/shard_map/concatenate | solution.py:20
  69.5 3.5 collective-permute-start.4
  75.3 4.2 copy.225
  91.7 3.9 collective-permute-done.13
  95.6 5.9 %collective-permute-start.14 = (f32[3,8,4,1,128]{4,1,3,2,0:T(8,128)S(1)}, f32[3,8,4,1,128]{4,1,3,2,0:T(8,128)S(1)}, u32[]{:S(2)}, u32[]{:S(2)}) collective-permute-start(f32[3,8,4,1,128]{4,1,3,2,0:T(8,128)S(1)} %get-tuple-element.76), channel_id=1, source_target_pairs={{0,8},{8,16},{16,24},{24,32},{32,40},{40,48},{48,56},{1,9},{9,17},... | collective-permute-start | bytes 147464 | tf_op jit(solution)/shard_map/ppermute | solution.py:16
  103.5 3.5 collective-permute-done.15
  107.2 4.9 collective-permute-start.16
  113.4 7.9 %collective-permute-done.16 = f32[3,8,4,10,1]{4,1,3,2,0:T(8,128)S(1)} collective-permute-done((f32[3,8,4,10,1]{4,1,3,2,0:T(8,128)S(1)}, f32[3,8,4,10,1]{4,1,3,2,0:T(8,128)S(1)}, u32[]{:S(2)}, u32[]{:S(2)}) %collective-permute-start.16) | collective-permute-done | bytes 3872 | tf_op jit(solution)/shard_map/ppermute | solution.py:16
  121.3 5.2 collective-permute-done.17
  132.5 4.1 collective-permute-done.19
  136.7 5.3 collective-permute-start.20
  143.9 3.5 collective-permute-done.21
  147.6 3.7 collective-permute-start.22
  152.8 7.7 %collective-permute-done.22 = f32[3,8,4,10,1]{4,1,3,2,0:T(8,128)S(1)} collective-permute-done((f32[3,8,4,10,1]{4,1,3,2,0:T(8,128)S(1)}, f32[3,8,4,10,1]{4,1,3,2,0:T(8,128)S(1)}, u32[]{:S(2)}, u32[]{:S(2)}) %collective-permute-start.22) | collective-permute-done | bytes 3872 | tf_op jit(solution)/shard_map/ppermute | solution.py:16
  160.5 4.1 collective-permute-done.23
  169.6 4.1 collective-permute-done.25
  173.7 4.8 collective-permute-start.26
  184.2 4.6 collective-permute-start.28
  190.4 7.6 %collective-permute-done.28 = f32[3,8,4,10,1]{4,1,3,2,0:T(8,128)S(1)} collective-permute-done((f32[3,8,4,10,1]{4,1,3,2,0:T(8,128)S(1)}, f32[3,8,4,10,1]{4,1,3,2,0:T(8,128)S(1)}, u32[]{:S(2)}, u32[]{:S(2)}) %collective-permute-start.28) | collective-permute-done | bytes 3872 | tf_op jit(solution)/shard_map/ppermute | solution.py:16
  198.0 4.1 collective-permute-done.29
  203.5 73.7 %all-reduce.3 = (f32[128,8]{0,1:T(8,128)S(1)}, f32[128,8]{0,1:T(8,128)S(1)}, f32[128,8]{0,1:T(8,128)S(1)}, f32[128,8]{0,1:T(8,128)S(1)}) all-reduce(f32[128,8]{0,1:T(8,128)S(1)} %fusion.25, f32[128,8]{0,1:T(8,128)S(1)} %fusion.13, f32[128,8]{0,1:T(8,128)S(1)} %fusion.17, ...), channel_id=1, replica_groups=mesh['gx'=4,'gy'=8,'gz'=8] {'gx','gy','gz'}, use_global_device_ids=true, to_apply=%region_0.0 | all-reduce | flops 4096 | bytes 32768 | tf_op jit(solution)/shard_map/psum | solution.py:79
  281.4 73.0 %all-reduce.2 = (f32[8,8]{0,1:T(8,128)S(1)}, f32[8,8]{0,1:T(8,128)S(1)}, f32[8,8]{0,1:T(8,128)S(1)}, f32[8,8]{0,1:T(8,128)S(1)}) all-reduce(f32[8,8]{0,1:T(8,128)S(1)} %fusion.33, f32[8,8]{0,1:T(8,128)S(1)} %fusion.29, f32[8,8]{0,1:T(8,128)S(1)} %fusion.30, f32[8,8]{0,1:T(8,128)S(1)} %fusion.31), channel_id=1, replica_groups=mesh['gx'=4,'gy'=8,'gz'=8] {'gx','gy','gz'}, use_global_device_ids=true, to_apply=%region_1.0 | all-reduce | flops 256 | bytes 2048 | tf_op jit(solution)/shard_map/psum | solution.py:81
  368.8 74.7 %all-reduce.1 = (f32[128,8]{0,1:T(8,128)S(1)}, f32[128,8]{0,1:T(8,128)S(1)}, f32[128,8]{0,1:T(8,128)S(1)}, f32[128,8]{0,1:T(8,128)S(1)}) all-reduce(f32[128,8]{0,1:T(8,128)S(1)} %fusion.23, f32[128,8]{0,1:T(8,128)S(1)} %fusion.11, f32[128,8]{0,1:T(8,128)S(1)} %fusion.15, ...), channel_id=1, replica_groups=mesh['gx'=4,'gy'=8,'gz'=8] {'gx','gy','gz'}, use_global_device_ids=true, to_apply=%region_4.0 | all-reduce | flops 4096 | bytes 32768 | tf_op jit(solution)/shard_map/psum | solution.py:84
  447.7 73.6 %all-reduce = (f32[8,8]{0,1:T(8,128)S(1)}, f32[8,8]{0,1:T(8,128)S(1)}, f32[8,8]{0,1:T(8,128)S(1)}, f32[8,8]{0,1:T(8,128)S(1)}) all-reduce(f32[8,8]{0,1:T(8,128)S(1)} %fusion.32, f32[8,8]{0,1:T(8,128)S(1)} %fusion.26, f32[8,8]{0,1:T(8,128)S(1)} %fusion.27, f32[8,8]{0,1:T(8,128)S(1)} %fusion.28), channel_id=1, replica_groups=mesh['gx'=4,'gy'=8,'gz'=8] {'gx','gy','gz'}, use_global_device_ids=true, to_apply=%region_5.0 | all-reduce | flops 256 | bytes 2048 | tf_op jit(solution)/shard_map/psum | solution.py:88
  (208 shorter events, 106.6 us)
Async XLA Ops:
  0.6 7.2 %copy-start = (bf16[2,3,8,128,128]{4,3,2,1,0:T(8,128)(2,1)S(1)}, bf16[2,3,8,128,128]{4,3,2,1,0:T(8,128)(2,1)}, u32[]{:S(2)}) copy-start(bf16[2,3,8,128,128]{4,3,2,1,0:T(8,128)(2,1)} %param.10) | copy-start | bytes 4718596
  2.5 23.6 %collective-permute-start = (f32[11,2,8,128]{3,2,1,0:T(8,128)S(1)}, f32[11,2,8,128]{3,2,1,0:T(8,128)S(1)}, u32[]{:S(2)}, u32[]{:S(2)}) collective-permute-start(f32[11,2,8,128]{3,2,1,0:T(8,128)S(1)} %pad_maximum_fusion.10), channel_id=1, source_target_pairs={{0,64},{64,128},{128,192},{1,65},{65,129},{129,193},{2,66},{66,130... | collective-permute-start | bytes 270344 | tf_op jit(solution)/shard_map/ppermute | solution.py:16
  6.5 19.6 %collective-permute-start.1 = (f32[11,2,8,128]{3,2,1,0:T(8,128)S(1)}, f32[11,2,8,128]{3,2,1,0:T(8,128)S(1)}, u32[]{:S(2)}, u32[]{:S(2)}) collective-permute-start(f32[11,2,8,128]{3,2,1,0:T(8,128)S(1)} %pad_maximum_fusion.10), channel_id=1, source_target_pairs={{64,0},{128,64},{192,128},{65,1},{129,65},{193,129},{66,2},{130,66... | collective-permute-start | bytes 270344 | tf_op jit(solution)/shard_map/ppermute | solution.py:19
  9.1 5.6 %collective-permute-start.6 = (f32[3,8,1,8,128]{4,1,3,2,0:T(8,128)S(1)}, f32[3,8,1,8,128]{4,1,3,2,0:T(8,128)S(1)}, u32[]{:S(2)}, u32[]{:S(2)}) collective-permute-start(f32[3,8,1,8,128]{4,1,3,2,0:T(8,128)S(1)} %copy.383), channel_id=1, source_target_pairs={{0,64},{64,128},{128,192},{1,65},{65,129},{129,193},{2,66},{66,130... | collective-permute-start | bytes 294920 | tf_op jit(solution)/shard_map/ppermute | solution.py:16
  13.1 5.4 collective-permute-start.7
  18.5 7.7 %collective-permute-start.8 = (f32[3,8,4,1,128]{4,1,3,2,0:T(8,128)S(1)}, f32[3,8,4,1,128]{4,1,3,2,0:T(8,128)S(1)}, u32[]{:S(2)}, u32[]{:S(2)}) collective-permute-start(f32[3,8,4,1,128]{4,1,3,2,0:T(8,128)S(1)} %get-tuple-element.78), channel_id=1, source_target_pairs={{0,8},{8,16},{16,24},{24,32},{32,40},{40,48},{48,56},{1,9},{9,17},... | collective-permute-start | bytes 147464 | tf_op jit(solution)/shard_map/ppermute | solution.py:16
  24.2 5.4 %collective-permute-start.9 = (f32[3,8,4,1,128]{4,1,3,2,0:T(8,128)S(1)}, f32[3,8,4,1,128]{4,1,3,2,0:T(8,128)S(1)}, u32[]{:S(2)}, u32[]{:S(2)}) collective-permute-start(f32[3,8,4,1,128]{4,1,3,2,0:T(8,128)S(1)} %get-tuple-element.79), channel_id=1, source_target_pairs={{8,0},{16,8},{24,16},{32,24},{40,32},{48,40},{56,48},{9,1},{17,9},... | collective-permute-start | bytes 147464 | tf_op jit(solution)/shard_map/ppermute | solution.py:19
  30.7 14.4 %collective-permute-start.10 = (f32[3,8,4,10,1]{4,1,3,2,0:T(8,128)}, f32[3,8,4,10,1]{4,1,3,2,0:T(8,128)S(1)}, u32[]{:S(2)}, u32[]{:S(2)}) collective-permute-start(f32[3,8,4,10,1]{4,1,3,2,0:T(8,128)} %get-tuple-element.70), channel_id=1, source_target_pairs={{0,1},{1,2},{2,3},{3,4},{4,5},{5,6},{6,7},{8,9},{9,10},{10,11},{11... | collective-permute-start | bytes 11528 | tf_op jit(solution)/shard_map/ppermute | solution.py:16
  34.3 13.6 %collective-permute-start.11 = (f32[3,8,4,10,1]{4,1,3,2,0:T(8,128)}, f32[3,8,4,10,1]{4,1,3,2,0:T(8,128)}, u32[]{:S(2)}, u32[]{:S(2)}) collective-permute-start(f32[3,8,4,10,1]{4,1,3,2,0:T(8,128)} %get-tuple-element.71), channel_id=1, source_target_pairs={{1,0},{2,1},{3,2},{4,3},{5,4},{6,5},{7,6},{9,8},{10,9},{11,10},{12... | collective-permute-start | bytes 11528 | tf_op jit(solution)/shard_map/ppermute | solution.py:19
  39.5 10.1 %collective-permute-start.2 = (f32[11,6,2,128]{3,1,2,0:T(8,128)S(1)}, f32[11,6,2,128]{3,1,2,0:T(8,128)}, u32[]{:S(2)}, u32[]{:S(2)}) collective-permute-start(f32[11,6,2,128]{3,1,2,0:T(8,128)S(1)} %copy.326), channel_id=1, source_target_pairs={{0,8},{8,16},{16,24},{24,32},{32,40},{40,48},{48,56},{1,9},{9,17},... | collective-permute-start | bytes 202760 | tf_op jit(solution)/shard_map/ppermute | solution.py:16
  42.3 11.8 %collective-permute-start.3 = (f32[11,6,2,128]{3,1,2,0:T(8,128)}, f32[11,6,2,128]{3,1,2,0:T(8,128)S(1)}, u32[]{:S(2)}, u32[]{:S(2)}) collective-permute-start(f32[11,6,2,128]{3,1,2,0:T(8,128)} %copy.327), channel_id=1, source_target_pairs={{8,0},{16,8},{24,16},{32,24},{40,32},{48,40},{56,48},{9,1},{17,9},... | collective-permute-start | bytes 202760 | tf_op jit(solution)/shard_map/ppermute | solution.py:19
  69.5 10.0 %collective-permute-start.4 = (f32[11,6,12,2]{2,1,3,0:T(8,128)S(1)}, f32[11,6,12,2]{2,1,3,0:T(8,128)S(1)}, u32[]{:S(2)}, u32[]{:S(2)}) collective-permute-start(f32[11,6,12,2]{2,1,3,0:T(8,128)S(1)} %get-tuple-element.44), channel_id=1, source_target_pairs={{0,1},{1,2},{2,3},{3,4},{4,5},{5,6},{6,7},{8,9},{9,10},{10,11},{11... | collective-permute-start | bytes 19016 | tf_op jit(solution)/shard_map/ppermute | solution.py:16
  73.1 7.0 %collective-permute-start.5 = (f32[11,6,12,2]{2,1,3,0:T(8,128)S(1)}, f32[11,6,12,2]{2,1,3,0:T(8,128)S(1)}, u32[]{:S(2)}, u32[]{:S(2)}) collective-permute-start(f32[11,6,12,2]{2,1,3,0:T(8,128)S(1)} %get-tuple-element.45), channel_id=1, source_target_pairs={{1,0},{2,1},{3,2},{4,3},{5,4},{6,5},{7,6},{9,8},{10,9},{11,10},{12... | collective-permute-start | bytes 19016 | tf_op jit(solution)/shard_map/ppermute | solution.py:19
  81.4 4.3 copy-start.4
  86.2 5.6 %collective-permute-start.12 = (f32[3,8,1,8,128]{4,1,3,2,0:T(8,128)S(1)}, f32[3,8,1,8,128]{4,1,3,2,0:T(8,128)S(1)}, u32[]{:S(2)}, u32[]{:S(2)}) collective-permute-start(f32[3,8,1,8,128]{4,1,3,2,0:T(8,128)S(1)} %get-tuple-element.86), channel_id=1, source_target_pairs={{0,64},{64,128},{128,192},{1,65},{65,129},{129,193},{2,66},{66,130... | collective-permute-start | bytes 294920 | tf_op jit(solution)/shard_map/ppermute | solution.py:16
  89.4 6.2 %collective-permute-start.13 = (f32[3,8,1,8,128]{4,1,3,2,0:T(8,128)S(1)}, f32[3,8,1,8,128]{4,1,3,2,0:T(8,128)S(1)}, u32[]{:S(2)}, u32[]{:S(2)}) collective-permute-start(f32[3,8,1,8,128]{4,1,3,2,0:T(8,128)S(1)} %get-tuple-element.87), channel_id=1, source_target_pairs={{64,0},{128,64},{192,128},{65,1},{129,65},{193,129},{66,2},{130,66... | collective-permute-start | bytes 294920 | tf_op jit(solution)/shard_map/ppermute | solution.py:19
  95.6 7.9 %collective-permute-start.14 = (f32[3,8,4,1,128]{4,1,3,2,0:T(8,128)S(1)}, f32[3,8,4,1,128]{4,1,3,2,0:T(8,128)S(1)}, u32[]{:S(2)}, u32[]{:S(2)}) collective-permute-start(f32[3,8,4,1,128]{4,1,3,2,0:T(8,128)S(1)} %get-tuple-element.76), channel_id=1, source_target_pairs={{0,8},{8,16},{16,24},{24,32},{32,40},{40,48},{48,56},{1,9},{9,17},... | collective-permute-start | bytes 147464 | tf_op jit(solution)/shard_map/ppermute | solution.py:16
  101.6 5.4 %collective-permute-start.15 = (f32[3,8,4,1,128]{4,1,3,2,0:T(8,128)S(1)}, f32[3,8,4,1,128]{4,1,3,2,0:T(8,128)S(1)}, u32[]{:S(2)}, u32[]{:S(2)}) collective-permute-start(f32[3,8,4,1,128]{4,1,3,2,0:T(8,128)S(1)} %get-tuple-element.77), channel_id=1, source_target_pairs={{8,0},{16,8},{24,16},{32,24},{40,32},{48,40},{56,48},{9,1},{17,9},... | collective-permute-start | bytes 147464 | tf_op jit(solution)/shard_map/ppermute | solution.py:19
  107.2 14.1 %collective-permute-start.16 = (f32[3,8,4,10,1]{4,1,3,2,0:T(8,128)S(1)}, f32[3,8,4,10,1]{4,1,3,2,0:T(8,128)S(1)}, u32[]{:S(2)}, u32[]{:S(2)}) collective-permute-start(f32[3,8,4,10,1]{4,1,3,2,0:T(8,128)S(1)} %get-tuple-element.68), channel_id=1, source_target_pairs={{0,1},{1,2},{2,3},{3,4},{4,5},{5,6},{6,7},{8,9},{9,10},{10,11},{11... | collective-permute-start | bytes 11528 | tf_op jit(solution)/shard_map/ppermute | solution.py:16
  112.1 14.4 %collective-permute-start.17 = (f32[3,8,4,10,1]{4,1,3,2,0:T(8,128)S(1)}, f32[3,8,4,10,1]{4,1,3,2,0:T(8,128)S(1)}, u32[]{:S(2)}, u32[]{:S(2)}) collective-permute-start(f32[3,8,4,10,1]{4,1,3,2,0:T(8,128)S(1)} %get-tuple-element.69), channel_id=1, source_target_pairs={{1,0},{2,1},{3,2},{4,3},{5,4},{6,5},{7,6},{9,8},{10,9},{11,10},{12... | collective-permute-start | bytes 11528 | tf_op jit(solution)/shard_map/ppermute | solution.py:19
  127.7 4.8 collective-permute-start.18
  130.7 6.0 %collective-permute-start.19 = (f32[3,8,1,8,128]{4,1,3,2,0:T(8,128)S(1)}, f32[3,8,1,8,128]{4,1,3,2,0:T(8,128)S(1)}, u32[]{:S(2)}, u32[]{:S(2)}) collective-permute-start(f32[3,8,1,8,128]{4,1,3,2,0:T(8,128)S(1)} %copy.386), channel_id=1, source_target_pairs={{64,0},{128,64},{192,128},{65,1},{129,65},{193,129},{66,2},{130,66... | collective-permute-start | bytes 294920 | tf_op jit(solution)/shard_map/ppermute | solution.py:19
  136.7 7.2 %collective-permute-start.20 = (f32[3,8,4,1,128]{4,1,3,2,0:T(8,128)S(1)}, f32[3,8,4,1,128]{4,1,3,2,0:T(8,128)S(1)}, u32[]{:S(2)}, u32[]{:S(2)}) collective-permute-start(f32[3,8,4,1,128]{4,1,3,2,0:T(8,128)S(1)} %get-tuple-element.74), channel_id=1, source_target_pairs={{0,8},{8,16},{16,24},{24,32},{32,40},{40,48},{48,56},{1,9},{9,17},... | collective-permute-start | bytes 147464 | tf_op jit(solution)/shard_map/ppermute | solution.py:16
  142.0 5.4 %collective-permute-start.21 = (f32[3,8,4,1,128]{4,1,3,2,0:T(8,128)S(1)}, f32[3,8,4,1,128]{4,1,3,2,0:T(8,128)S(1)}, u32[]{:S(2)}, u32[]{:S(2)}) collective-permute-start(f32[3,8,4,1,128]{4,1,3,2,0:T(8,128)S(1)} %get-tuple-element.75), channel_id=1, source_target_pairs={{8,0},{16,8},{24,16},{32,24},{40,32},{48,40},{56,48},{9,1},{17,9},... | collective-permute-start | bytes 147464 | tf_op jit(solution)/shard_map/ppermute | solution.py:19
  147.6 12.9 %collective-permute-start.22 = (f32[3,8,4,10,1]{4,1,3,2,0:T(8,128)S(1)}, f32[3,8,4,10,1]{4,1,3,2,0:T(8,128)S(1)}, u32[]{:S(2)}, u32[]{:S(2)}) collective-permute-start(f32[3,8,4,10,1]{4,1,3,2,0:T(8,128)S(1)} %get-tuple-element.66), channel_id=1, source_target_pairs={{0,1},{1,2},{2,3},{3,4},{4,5},{5,6},{6,7},{8,9},{9,10},{10,11},{11... | collective-permute-start | bytes 11528 | tf_op jit(solution)/shard_map/ppermute | solution.py:16
  151.3 13.3 %collective-permute-start.23 = (f32[3,8,4,10,1]{4,1,3,2,0:T(8,128)S(1)}, f32[3,8,4,10,1]{4,1,3,2,0:T(8,128)S(1)}, u32[]{:S(2)}, u32[]{:S(2)}) collective-permute-start(f32[3,8,4,10,1]{4,1,3,2,0:T(8,128)S(1)} %get-tuple-element.67), channel_id=1, source_target_pairs={{1,0},{2,1},{3,2},{4,3},{5,4},{6,5},{7,6},{9,8},{10,9},{11,10},{12... | collective-permute-start | bytes 11528 | tf_op jit(solution)/shard_map/ppermute | solution.py:19
  165.8 3.8 collective-permute-start.24
  167.7 6.0 %collective-permute-start.25 = (f32[3,8,1,8,128]{4,1,3,2,0:T(8,128)S(1)}, f32[3,8,1,8,128]{4,1,3,2,0:T(8,128)S(1)}, u32[]{:S(2)}, u32[]{:S(2)}) collective-permute-start(f32[3,8,1,8,128]{4,1,3,2,0:T(8,128)S(1)} %get-tuple-element.83), channel_id=1, source_target_pairs={{64,0},{128,64},{192,128},{65,1},{129,65},{193,129},{66,2},{130,66... | collective-permute-start | bytes 294920 | tf_op jit(solution)/shard_map/ppermute | solution.py:19
  173.7 7.0 %collective-permute-start.26 = (f32[3,8,4,1,128]{4,1,3,2,0:T(8,128)S(1)}, f32[3,8,4,1,128]{4,1,3,2,0:T(8,128)S(1)}, u32[]{:S(2)}, u32[]{:S(2)}) collective-permute-start(f32[3,8,4,1,128]{4,1,3,2,0:T(8,128)S(1)} %get-tuple-element.72), channel_id=1, source_target_pairs={{0,8},{8,16},{16,24},{24,32},{32,40},{40,48},{48,56},{1,9},{9,17},... | collective-permute-start | bytes 147464 | tf_op jit(solution)/shard_map/ppermute | solution.py:16
  178.5 5.4 %collective-permute-start.27 = (f32[3,8,4,1,128]{4,1,3,2,0:T(8,128)S(1)}, f32[3,8,4,1,128]{4,1,3,2,0:T(8,128)S(1)}, u32[]{:S(2)}, u32[]{:S(2)}) collective-permute-start(f32[3,8,4,1,128]{4,1,3,2,0:T(8,128)S(1)} %get-tuple-element.73), channel_id=1, source_target_pairs={{8,0},{16,8},{24,16},{32,24},{40,32},{48,40},{56,48},{9,1},{17,9},... | collective-permute-start | bytes 147464 | tf_op jit(solution)/shard_map/ppermute | solution.py:19
  184.2 13.8 %collective-permute-start.28 = (f32[3,8,4,10,1]{4,1,3,2,0:T(8,128)S(1)}, f32[3,8,4,10,1]{4,1,3,2,0:T(8,128)S(1)}, u32[]{:S(2)}, u32[]{:S(2)}) collective-permute-start(f32[3,8,4,10,1]{4,1,3,2,0:T(8,128)S(1)} %get-tuple-element.64), channel_id=1, source_target_pairs={{0,1},{1,2},{2,3},{3,4},{4,5},{5,6},{6,7},{8,9},{9,10},{10,11},{11... | collective-permute-start | bytes 11528 | tf_op jit(solution)/shard_map/ppermute | solution.py:16
  188.8 13.3 %collective-permute-start.29 = (f32[3,8,4,10,1]{4,1,3,2,0:T(8,128)S(1)}, f32[3,8,4,10,1]{4,1,3,2,0:T(8,128)S(1)}, u32[]{:S(2)}, u32[]{:S(2)}) collective-permute-start(f32[3,8,4,10,1]{4,1,3,2,0:T(8,128)S(1)} %get-tuple-element.65), channel_id=1, source_target_pairs={{1,0},{2,1},{3,2},{4,3},{5,4},{6,5},{7,6},{9,8},{10,9},{11,10},{12... | collective-permute-start | bytes 11528 | tf_op jit(solution)/shard_map/ppermute | solution.py:19
  (3 other events, 7.5 us)
where the time goes:
time: 540 us; the launch traced here: 538 us
  blocking collectives  295 us (55%)
  starting transfers between devices  83.7 us (16%)
  waiting for transfers between devices  70.1 us (13%)
  other arithmetic  38.1 us (7%)
  local copies, waits for them, and re-layouts  27.4 us (5%)
  matrix products  22 us (4%)
    psum x1, blocking collectives, orthonormalize(): lax.psum(project(basis, first_q.astype(jnp.bfloat16)) * dof_weight, ('gx'...  74.7 us
    psum x1, blocking collectives, orthonormalize(): first_coef = lax.psum(partial_coef, ('gx', 'gy', 'gz'))  73.7 us
    psum x1, blocking collectives, orthonormalize(): lax.psum(local_gram(second_resid) * dof_weight, ('gx', 'gy', 'gz'))  73.6 us
    psum x1, blocking collectives, orthonormalize(): lax.psum(local_gram(first_resid) * dof_weight, ('gx', 'gy', 'gz'))  73 us
    ppermute x15, starting transfers between devices, padded_2(): lax.ppermute(lax.slice_in_dim(block, block.shape[dim] - width, None, axis...  60.2 us
    ppermute x15, waiting for transfers between devices, padded_2(): lax.ppermute(lax.slice_in_dim(block, 0, width, axis=dim), axis, backward)  44.8 us
    ppermute x15, waiting for transfers between devices, padded_2(): lax.ppermute(lax.slice_in_dim(block, block.shape[dim] - width, None, axis...  25.3 us
    ppermute x15, starting transfers between devices, padded_2(): lax.ppermute(lax.slice_in_dim(block, 0, width, axis=dim), axis, backward)  23.6 us
  transfers between devices with their start and end apart: 30, of which 19 were waited for; matrix products, arithmetic and copies ran while one was open for 3% of the time, Pallas kernels for 0%

commit v1 on v0

--- a/solution.py
+++ b/solution.py
@@ -81,8 +81,11 @@
     first_gram = lax.psum(local_gram(first_resid) * dof_weight, ("gx", "gy", "gz"))
     first_lower = jnp.linalg.cholesky(first_gram)
     first_q = apply_inverse(first_resid, first_lower)
-    second_coef = lax.psum(
-        project(basis, first_q.astype(jnp.bfloat16)) * dof_weight, ("gx", "gy", "gz")
+    second_coef = jnp.sum(
+        lax.all_gather(
+            project(basis, first_q.astype(jnp.bfloat16)) * dof_weight, ("gx", "gy", "gz")
+        ),
+        axis=0,
     )
     second_resid = first_q - expand(basis, second_coef.astype(jnp.bfloat16))
     second_gram = lax.psum(local_gram(second_resid) * dof_weight, ("gx", "gy", "gz"))

time: 540 us -> 884 us (1.64)
  waiting for transfers between devices: 70.1 us -> 464 us
  blocking collectives: 295 us -> 224 us
  between operations: 1.47 us -> 14.6 us
    all_gather x0 -> x4, waiting for transfers between devices: none -> 394 us  [orthonormalize(): lax.all_gather(project(basis, first_q.astype(jnp.bfloat16)) * dof_weight,...]
    psum x1 -> x0, blocking collectives: 74.7 us -> none  [orthonormalize(): lax.psum(project(basis, first_q.astype(jnp.bfloat16)) * dof_weight, ('gx'...]
  transfers between devices with their start and end apart: 30 -> 34, of which waited for: 19 -> 23; matrix products, arithmetic and copies ran while one was open for 3% -> 4% of each run, Pallas kernels for 0% -> 0%
where the time goes in v1:
time: 884 us; the launch traced here: 882 us
  waiting for transfers between devices  464 us (52%)
  blocking collectives  224 us (25%)
  starting transfers between devices  84 us (10%)
  other arithmetic  44 us (5%)
  local copies, waits for them, and re-layouts  27.4 us (3%)
  matrix products  24.3 us (3%)
  between operations  14.6 us (2%)
    all_gather x4, waiting for transfers between devices, orthonormalize(): lax.all_gather(project(basis, first_q.astype(jnp.bfloat16)) * dof_weight,...  394 us
    psum x1, blocking collectives, orthonormalize(): lax.psum(local_gram(second_resid) * dof_weight, ('gx', 'gy', 'gz'))  77 us
    psum x1, blocking collectives, orthonormalize(): first_coef = lax.psum(partial_coef, ('gx', 'gy', 'gz'))  73.7 us
    psum x1, blocking collectives, orthonormalize(): lax.psum(local_gram(first_resid) * dof_weight, ('gx', 'gy', 'gz'))  73 us
    ppermute x15, starting transfers between devices, padded_2(): lax.ppermute(lax.slice_in_dim(block, block.shape[dim] - width, None, axis...  60.1 us
    ppermute x15, waiting for transfers between devices, padded_2(): lax.ppermute(lax.slice_in_dim(block, 0, width, axis=dim), axis, backward)  44.9 us
    ppermute x15, waiting for transfers between devices, padded_2(): lax.ppermute(lax.slice_in_dim(block, block.shape[dim] - width, None, axis...  25.3 us
    ppermute x15, starting transfers between devices, padded_2(): lax.ppermute(lax.slice_in_dim(block, 0, width, axis=dim), axis, backward)  23.6 us
  transfers between devices with their start and end apart: 34, of which 23 were waited for; matrix products, arithmetic and copies ran while one was open for 4% of the time, Pallas kernels for 0%

profile of v1, /device:TPU:1, one launch (start us, length us, event | category | flops | bytes accessed | tf_op | source)
XLA Modules:
  0.0 882.0 jit_solution(14951427481508531063)
XLA Ops:
  9.1 4.0 collective-permute-start
  15.7 4.0 collective-permute-start.6
  21.3 3.7 collective-permute-done.7
  25.1 5.7 collective-permute-start.8
  37.3 3.6 collective-permute-start.10
  42.2 3.8 copy.222
  56.1 4.5 copy.221
  60.7 3.9 copy.223
  64.6 9.0 %pad_maximum_fusion = f32[11,6,12,128]{2,1,3,0:T(8,128)S(1)} fusion(f32[11,6,2,128]{2,1,3,0:T(8,128)} %copy.223, f32[11,6,8,128]{2,1,3,0:T(8,128)} %copy.222, f32[11,6,2,128]{2,1,3,0:T(8,128)} %copy.221), kind=kLoop, calls=%fused_computation | loop fusion | flops 202752 | bytes 811008 | tf_op jit(solution)/shard_map/concatenate | solution.py:20
  81.8 4.2 copy.225
  98.3 3.9 collective-permute-done.13
  102.2 5.9 collective-permute-start.14
  113.8 4.9 collective-permute-start.16
  120.0 7.9 collective-permute-done.16
  127.9 5.2 collective-permute-done.17
  139.1 4.1 collective-permute-done.19
  143.2 5.3 collective-permute-start.20
  154.2 3.7 collective-permute-start.22
  159.3 7.7 collective-permute-done.22
  167.0 4.1 collective-permute-done.23
  176.2 4.1 collective-permute-done.25
  180.3 4.8 collective-permute-start.26
  190.7 4.6 collective-permute-start.28
  196.9 7.6 collective-permute-done.28
  204.5 4.1 collective-permute-done.29
  210.1 73.7 %all-reduce.2 = (f32[128,8]{0,1:T(8,128)S(1)}, f32[128,8]{0,1:T(8,128)S(1)}, f32[128,8]{0,1:T(8,128)S(1)}, f32[128,8]{0,1:T(8,128)S(1)}) all-reduce(f32[128,8]{0,1:T(8,128)S(1)} %fusion.25, f32[128,8]{0,1:T(8,128)S(1)} %fusion.13, f32[128,8]{0,1:T(8,128)S(1)} %fusion.17, ...), channel_id=1, replica_groups=mesh['gx'=4,'gy'=8,'gz'=8] {'gx','gy','gz'}, use_global_device_ids=true, to_apply=%region_0.0 | all-reduce | flops 4096 | bytes 32768 | tf_op jit(solution)/shard_map/psum | solution.py:79
  288.0 73.0 %all-reduce.1 = (f32[8,8]{0,1:T(8,128)S(1)}, f32[8,8]{0,1:T(8,128)S(1)}, f32[8,8]{0,1:T(8,128)S(1)}, f32[8,8]{0,1:T(8,128)S(1)}) all-reduce(f32[8,8]{0,1:T(8,128)S(1)} %fusion.33, f32[8,8]{0,1:T(8,128)S(1)} %fusion.29, f32[8,8]{0,1:T(8,128)S(1)} %fusion.30, f32[8,8]{0,1:T(8,128)S(1)} %fusion.31), channel_id=1, replica_groups=mesh['gx'=4,'gy'=8,'gz'=8] {'gx','gy','gz'}, use_global_device_ids=true, to_apply=%region_1.0 | all-reduce | flops 256 | bytes 2048 | tf_op jit(solution)/shard_map/psum | solution.py:81
  379.0 85.5 %all-gather.11.cloned.1.call-done = f32[32768,8]{0,1:T(8,128)} async-done(((f32[128,8]{0,1:T(8,128)}), f32[32768,8]{0,1:T(8,128)}) %all-gather.11.cloned.1.call-update) | async-done | bytes 1048592 | tf_op jit(solution)/shard_map/all_gather | solution.py:85
  466.0 103.8 %all-gather.13.cloned.1.call-done = f32[32768,8]{0,1:T(8,128)} async-done(((f32[128,8]{0,1:T(8,128)}), f32[32768,8]{0,1:T(8,128)}) %all-gather.13.cloned.1.call-update) | async-done | bytes 1048592 | tf_op jit(solution)/shard_map/all_gather | solution.py:85
  571.3 103.8 %all-gather.15.cloned.1.call-done = f32[32768,8]{0,1:T(8,128)} async-done(((f32[128,8]{0,1:T(8,128)}), f32[32768,8]{0,1:T(8,128)}) %all-gather.15.cloned.1.call-update) | async-done | bytes 1048592 | tf_op jit(solution)/shard_map/all_gather | solution.py:85
  679.8 100.5 %all-gather.9.cloned.1.call-done = f32[32768,8]{0,1:T(8,128)} async-done(((f32[128,8]{0,1:T(8,128)}), f32[32768,8]{0,1:T(8,128)}) %all-gather.9.cloned.1.call-update) | async-done | bytes 1048592 | tf_op jit(solution)/shard_map/all_gather | solution.py:85
  782.9 77.0 %all-reduce = (f32[8,8]{0,1:T(8,128)S(1)}, f32[8,8]{0,1:T(8,128)S(1)}, f32[8,8]{0,1:T(8,128)S(1)}, f32[8,8]{0,1:T(8,128)S(1)}) all-reduce(f32[8,8]{0,1:T(8,128)S(1)} %fusion.32, f32[8,8]{0,1:T(8,128)S(1)} %fusion.26, f32[8,8]{0,1:T(8,128)S(1)} %fusion.27, f32[8,8]{0,1:T(8,128)S(1)} %fusion.28), channel_id=1, replica_groups=mesh['gx'=4,'gy'=8,'gz'=8] {'gx','gy','gz'}, use_global_device_ids=true, to_apply=%region_5.0 | all-reduce | flops 256 | bytes 2048 | tf_op jit(solution)/shard_map/psum | solution.py:91
  (223 shorter events, 125.6 us)
Async XLA Ops:
  7.2 457.3 %all-gather.11.cloned.1.call-start = ((), (), s32[]{:S(2)}) async-start(), calls=%async_computation.1 | async-start | bytes 1052672 | tf_op jit(solution)/shard_map/all_gather | solution.py:85
  9.1 23.6 %collective-permute-start = (f32[11,2,8,128]{3,2,1,0:T(8,128)S(1)}, f32[11,2,8,128]{3,2,1,0:T(8,128)S(1)}, u32[]{:S(2)}, u32[]{:S(2)}) collective-permute-start(f32[11,2,8,128]{3,2,1,0:T(8,128)S(1)} %pad_maximum_fusion.10), channel_id=1, source_target_pairs={{0,64},{64,128},{128,192},{1,65},{65,129},{129,193},{2,66},{66,130... | collective-permute-start | bytes 270344 | tf_op jit(solution)/shard_map/ppermute | solution.py:16
  13.1 19.6 %collective-permute-start.1 = (f32[11,2,8,128]{3,2,1,0:T(8,128)S(1)}, f32[11,2,8,128]{3,2,1,0:T(8,128)S(1)}, u32[]{:S(2)}, u32[]{:S(2)}) collective-permute-start(f32[11,2,8,128]{3,2,1,0:T(8,128)S(1)} %pad_maximum_fusion.10), channel_id=1, source_target_pairs={{64,0},{128,64},{192,128},{65,1},{129,65},{193,129},{66,2},{130,66... | collective-permute-start | bytes 270344 | tf_op jit(solution)/shard_map/ppermute | solution.py:19
  15.7 5.6 collective-permute-start.6
  19.7 5.4 collective-permute-start.7
  25.1 7.7 collective-permute-start.8
  30.7 5.4 collective-permute-start.9
  37.3 14.4 %collective-permute-start.10 = (f32[3,8,4,10,1]{4,1,3,2,0:T(8,128)}, f32[3,8,4,10,1]{4,1,3,2,0:T(8,128)S(1)}, u32[]{:S(2)}, u32[]{:S(2)}) collective-permute-start(f32[3,8,4,10,1]{4,1,3,2,0:T(8,128)} %get-tuple-element.66), channel_id=1, source_target_pairs={{0,1},{1,2},{2,3},{3,4},{4,5},{5,6},{6,7},{8,9},{9,10},{10,11},{11... | collective-permute-start | bytes 11528 | tf_op jit(solution)/shard_map/ppermute | solution.py:16
  40.9 13.6 %collective-permute-start.11 = (f32[3,8,4,10,1]{4,1,3,2,0:T(8,128)}, f32[3,8,4,10,1]{4,1,3,2,0:T(8,128)}, u32[]{:S(2)}, u32[]{:S(2)}) collective-permute-start(f32[3,8,4,10,1]{4,1,3,2,0:T(8,128)} %get-tuple-element.67), channel_id=1, source_target_pairs={{1,0},{2,1},{3,2},{4,3},{5,4},{6,5},{7,6},{9,8},{10,9},{11,10},{12... | collective-permute-start | bytes 11528 | tf_op jit(solution)/shard_map/ppermute | solution.py:19
  46.0 10.1 %collective-permute-start.2 = (f32[11,6,2,128]{3,1,2,0:T(8,128)S(1)}, f32[11,6,2,128]{3,1,2,0:T(8,128)}, u32[]{:S(2)}, u32[]{:S(2)}) collective-permute-start(f32[11,6,2,128]{3,1,2,0:T(8,128)S(1)} %copy.326), channel_id=1, source_target_pairs={{0,8},{8,16},{16,24},{24,32},{32,40},{40,48},{48,56},{1,9},{9,17},... | collective-permute-start | bytes 202760 | tf_op jit(solution)/shard_map/ppermute | solution.py:16
  48.9 11.8 %collective-permute-start.3 = (f32[11,6,2,128]{3,1,2,0:T(8,128)}, f32[11,6,2,128]{3,1,2,0:T(8,128)S(1)}, u32[]{:S(2)}, u32[]{:S(2)}) collective-permute-start(f32[11,6,2,128]{3,1,2,0:T(8,128)} %copy.327), channel_id=1, source_target_pairs={{8,0},{16,8},{24,16},{32,24},{40,32},{48,40},{56,48},{9,1},{17,9},... | collective-permute-start | bytes 202760 | tf_op jit(solution)/shard_map/ppermute | solution.py:19
  76.1 10.0 %collective-permute-start.4 = (f32[11,6,12,2]{2,1,3,0:T(8,128)S(1)}, f32[11,6,12,2]{2,1,3,0:T(8,128)S(1)}, u32[]{:S(2)}, u32[]{:S(2)}) collective-permute-start(f32[11,6,12,2]{2,1,3,0:T(8,128)S(1)} %get-tuple-element.40), channel_id=1, source_target_pairs={{0,1},{1,2},{2,3},{3,4},{4,5},{5,6},{6,7},{8,9},{9,10},{10,11},{11... | collective-permute-start | bytes 19016 | tf_op jit(solution)/shard_map/ppermute | solution.py:16
  79.6 7.0 collective-permute-start.5
  92.8 5.6 collective-permute-start.12
  96.0 6.3 collective-permute-start.13
  102.2 7.9 collective-permute-start.14
  108.2 5.4 collective-permute-start.15
  113.8 14.1 %collective-permute-start.16 = (f32[3,8,4,10,1]{4,1,3,2,0:T(8,128)S(1)}, f32[3,8,4,10,1]{4,1,3,2,0:T(8,128)S(1)}, u32[]{:S(2)}, u32[]{:S(2)}) collective-permute-start(f32[3,8,4,10,1]{4,1,3,2,0:T(8,128)S(1)} %get-tuple-element.64), channel_id=1, source_target_pairs={{0,1},{1,2},{2,3},{3,4},{4,5},{5,6},{6,7},{8,9},{9,10},{10,11},{11... | collective-permute-start | bytes 11528 | tf_op jit(solution)/shard_map/ppermute | solution.py:16
  118.7 14.4 %collective-permute-start.17 = (f32[3,8,4,10,1]{4,1,3,2,0:T(8,128)S(1)}, f32[3,8,4,10,1]{4,1,3,2,0:T(8,128)S(1)}, u32[]{:S(2)}, u32[]{:S(2)}) collective-permute-start(f32[3,8,4,10,1]{4,1,3,2,0:T(8,128)S(1)} %get-tuple-element.65), channel_id=1, source_target_pairs={{1,0},{2,1},{3,2},{4,3},{5,4},{6,5},{7,6},{9,8},{10,9},{11,10},{12... | collective-permute-start | bytes 11528 | tf_op jit(solution)/shard_map/ppermute | solution.py:19
  137.2 6.0 collective-permute-start.19
  143.2 7.2 collective-permute-start.20
  148.5 5.4 collective-permute-start.21
  154.2 12.9 %collective-permute-start.22 = (f32[3,8,4,10,1]{4,1,3,2,0:T(8,128)S(1)}, f32[3,8,4,10,1]{4,1,3,2,0:T(8,128)S(1)}, u32[]{:S(2)}, u32[]{:S(2)}) collective-permute-start(f32[3,8,4,10,1]{4,1,3,2,0:T(8,128)S(1)} %get-tuple-element.62), channel_id=1, source_target_pairs={{0,1},{1,2},{2,3},{3,4},{4,5},{5,6},{6,7},{8,9},{9,10},{10,11},{11... | collective-permute-start | bytes 11528 | tf_op jit(solution)/shard_map/ppermute | solution.py:16
  157.9 13.3 %collective-permute-start.23 = (f32[3,8,4,10,1]{4,1,3,2,0:T(8,128)S(1)}, f32[3,8,4,10,1]{4,1,3,2,0:T(8,128)S(1)}, u32[]{:S(2)}, u32[]{:S(2)}) collective-permute-start(f32[3,8,4,10,1]{4,1,3,2,0:T(8,128)S(1)} %get-tuple-element.63), channel_id=1, source_target_pairs={{1,0},{2,1},{3,2},{4,3},{5,4},{6,5},{7,6},{9,8},{10,9},{11,10},{12... | collective-permute-start | bytes 11528 | tf_op jit(solution)/shard_map/ppermute | solution.py:19
  174.3 6.0 collective-permute-start.25
  180.3 7.0 collective-permute-start.26
  185.1 5.4 collective-permute-start.27
  190.7 13.8 %collective-permute-start.28 = (f32[3,8,4,10,1]{4,1,3,2,0:T(8,128)S(1)}, f32[3,8,4,10,1]{4,1,3,2,0:T(8,128)S(1)}, u32[]{:S(2)}, u32[]{:S(2)}) collective-permute-start(f32[3,8,4,10,1]{4,1,3,2,0:T(8,128)S(1)} %get-tuple-element.60), channel_id=1, source_target_pairs={{0,1},{1,2},{2,3},{3,4},{4,5},{5,6},{6,7},{8,9},{9,10},{10,11},{11... | collective-permute-start | bytes 11528 | tf_op jit(solution)/shard_map/ppermute | solution.py:16
  195.3 13.3 %collective-permute-start.29 = (f32[3,8,4,10,1]{4,1,3,2,0:T(8,128)S(1)}, f32[3,8,4,10,1]{4,1,3,2,0:T(8,128)S(1)}, u32[]{:S(2)}, u32[]{:S(2)}) collective-permute-start(f32[3,8,4,10,1]{4,1,3,2,0:T(8,128)S(1)} %get-tuple-element.61), channel_id=1, source_target_pairs={{1,0},{2,1},{3,2},{4,3},{5,4},{6,5},{7,6},{9,8},{10,9},{11,10},{12... | collective-permute-start | bytes 11528 | tf_op jit(solution)/shard_map/ppermute | solution.py:19
  365.2 204.7 %all-gather.13.cloned.1.call-start = ((), (), s32[]{:S(2)}) async-start(), calls=%async_computation.2 | async-start | bytes 1052672 | tf_op jit(solution)/shard_map/all_gather | solution.py:85
  369.6 305.6 %all-gather.15.cloned.1.call-start = ((), (), s32[]{:S(2)}) async-start(), calls=%async_computation.3 | async-start | bytes 1052672 | tf_op jit(solution)/shard_map/all_gather | solution.py:85
  373.7 406.6 %all-gather.9.cloned.1.call-start = ((), (), s32[]{:S(2)}) async-start(), calls=%async_computation | async-start | bytes 1052672 | tf_op jit(solution)/shard_map/all_gather | solution.py:85
  (7 other events, 27.6 us)
Sparse Core Ops, SparseCore 0:
  365.3 99.1 all-gather.10
  468.8 100.9 all-gather.12
  574.1 100.9 all-gather.14
  679.3 100.9 all-gather.8
